TPU v7x, 128 devices: a whole 4x4x4 slice. The times are simulated.
128 devices in a mesh: rows: 32 (over x, z, core), feat: 4 (over y).
Axes of the slice: x: 4, y: 4, z: 4, core: 2. Of those that a mesh axis runs over, the one named last changes fastest.
Arguments:
- binned: int32 [65536, 256], P('rows', 'feat'), may hold values from 0 to 255
- node_index: int32 [65536, 1], P('rows'), may hold values from 0 to 31; in each aligned block of 2048 rows (0 to 2047, 2048 to 4095, ...) at most 128 rows name the same one
- treatment: float32 [65536], P('rows'), may hold values from -6 to 6
- outcome: float32 [65536], P('rows'), may hold values from -6 to 6
- unit_weight: float32 [65536], P('rows'), may hold values from 0.1 to 2
- root_feature: int32 [32], replicated, may hold values from 0 to 255
- root_cutoff: int32 [32], replicated, may hold values from 64 to 191
- child_feature: int32 [64], replicated, may hold values from 0 to 255
- child_cutoff: int32 [64], replicated, may hold values from 64 to 191
Outputs:
- node_moments: float32 [32, 3, 256, 256], P('rows', None, 'feat')
- child_moments: float32 [64, 3, 256, 256], P('rows', None, 'feat')
- leaf_moments: float32 [128, 3, 256, 256], P('rows', None, 'feat')
Inputs may be any that keep to these rules, and one draw needn't show every extreme that they name: `node_index`: among the rows of one device no node is named by more than 128 rows, a bound that some block reaches.
All inputs are finite; a program needn't handle non-finite values.
Results may differ from a plain program's by a relative error of at most 0.0022.
Values may be sent and summed in bfloat16 or wider, within the bound.
No kernel may reach another device: no remote copies, remote signals or barrier semaphores. Data moves between devices by JAX's collectives and lax.ppermute only.
A program may use at most 64 MiB of HBM per device.

v0:
```python
import jax
import jax.numpy as jnp
from jax import lax
from jax.sharding import PartitionSpec as P

BINS = 256


def histogram(weighted, features):
    feat_count, unit_count = features.shape
    blocks = features.reshape(feat_count // 4, 4, unit_count)
    levels = jnp.arange(BINS).astype(features.dtype)

    def one_block(carry, block):
        table = (block[:, :, None] == levels).astype(jnp.bfloat16)
        part = jnp.einsum("sc,fsb->cfb", weighted, table, preferred_element_type=jnp.float32)
        return (carry, part)

    unused, parts = lax.scan(one_block, 0, blocks)
    return jnp.moveaxis(parts, 0, 1).reshape(weighted.shape[1], feat_count, BINS)


def weigh(groups, group_count, moments):
    chosen = groups[:, None] == jnp.arange(group_count)
    spread = jnp.where(chosen[:, :, None], moments[:, None, :], jnp.zeros((), jnp.bfloat16))
    return spread.reshape(moments.shape[0], group_count * 3)


def on_device(
    binned,
    node_index,
    treatment,
    outcome,
    unit_weight,
    root_feature,
    root_cutoff,
    child_feature,
    child_cutoff,
):
    rows_here, feat_here = binned.shape
    node_count = root_feature.shape[0]
    owners = lax.axis_size("rows")
    per_owner = node_count // owners
    capacity = 2 * rows_here // node_count
    tree_node = node_index[:, 0]
    moments = jnp.stack(
        [unit_weight, unit_weight * treatment * treatment, unit_weight * treatment * outcome], 1
    ).astype(jnp.bfloat16)
    feature_major = binned.T
    first_child = 2 * tree_node
    wanted = jnp.stack(
        [root_feature[tree_node], child_feature[first_child], child_feature[first_child + 1]], 0
    )
    wanted = wanted - lax.axis_index("feat") * feat_here
    local_index = jnp.arange(feat_here)
    picked = jnp.sum(jnp.where(wanted[:, :, None] == local_index, binned[None, :, :], 0), axis=2)
    split_values = lax.psum(picked.astype(jnp.float32), "feat").astype(jnp.int32)
    right_root = (split_values[0] > root_cutoff[tree_node]).astype(jnp.int32)
    right_child = jnp.where(
        right_root == 1,
        split_values[2] > child_cutoff[first_child + 1],
        split_values[1] > child_cutoff[first_child],
    ).astype(jnp.int32)
    leaf_code = 2 * right_root + right_child
    all_weighted = weigh(tree_node, node_count, moments)
    all_terms = histogram(all_weighted, feature_major).reshape(node_count, 3, feat_here, BINS)
    node_moments = lax.psum_scatter(all_terms, "rows", scatter_dimension=0, tiled=True)
    node_onehot = (tree_node[:, None] == jnp.arange(node_count)).astype(jnp.int32)
    rank_in_node = jnp.sum(jnp.cumsum(node_onehot, 0) * node_onehot, 1) - 1
    slot_index = tree_node * capacity + rank_in_node
    feat_buffer = (
        jnp.zeros((feat_here, node_count * capacity), jnp.bfloat16)
        .at[:, slot_index]
        .set(feature_major.astype(jnp.bfloat16))
    )
    carried = jnp.concatenate([moments.T, leaf_code[None, :].astype(jnp.bfloat16)], 0)
    moment_buffer = (
        jnp.zeros((4, node_count * capacity), jnp.bfloat16).at[:, slot_index].set(carried)
    )
    feat_buffer = feat_buffer.reshape(feat_here, owners, per_owner * capacity)
    moment_buffer = moment_buffer.reshape(4, owners, per_owner * capacity)
    got_feat, got_moment = (
        lax.all_to_all(feat_buffer, "rows", split_axis=1, concat_axis=1, tiled=True),
        lax.all_to_all(moment_buffer, "rows", split_axis=1, concat_axis=1, tiled=True),
    )
    slots = owners * per_owner * capacity
    got_feat = got_feat.reshape(feat_here, slots)
    got_moment = got_moment.reshape(4, slots)
    owned_node = jnp.arange(slots) % (per_owner * capacity) // capacity
    got_leaf = got_moment[3].astype(jnp.int32)
    got_values = got_moment[:3].T
    leaf_weighted = weigh(4 * owned_node + got_leaf, 4 * per_owner, got_values)
    leaf_moments = histogram(leaf_weighted, got_feat).reshape(4 * per_owner, 3, feat_here, BINS)
    child_moments = leaf_moments.reshape(2 * per_owner, 2, 3, feat_here, BINS).sum(1)
    return (node_moments, child_moments, leaf_moments)


def solution(mesh):
    in_specs = (
        P("rows", "feat"),
        P("rows", None),
        P("rows"),
        P("rows"),
        P("rows"),
        P(),
        P(),
        P(),
        P(),
    )
    out_specs = (
        P("rows", None, "feat", None),
        P("rows", None, "feat", None),
        P("rows", None, "feat", None),
    )
    return jax.shard_map(
        on_device, mesh=mesh, in_specs=in_specs, out_specs=out_specs, check_vma=False
    )
```

profile of v0, /device:TPU:1, one launch (start us, length us, event | category | flops | bytes accessed | tf_op | source)
XLA Modules:
  0.0 438.4 jit_solution(8207467654154019221)
XLA Ops:
  10.0 59.8 %while.22 = (s32[]{:T(128)}, f32[16,96,4,256]{3,1,2,0:T(8,128)}, s32[16,4,2048]{2,1,0:T(4,128)S(1)}, bf16[2048,3]{0,1:T(4,128)(2,1)S(1)}, pred[2048,32]{0,1:T(8,128)(4,1)S(1)}, /*index=5*/s32[]{:T(128)}) while((s32[]{:T(128)}, f32[16,96,4,256]{3,1,2,0:T(8,128)}, s32[16,4,2048]{2,1,0:T(4,128)S(1)}, bf16[2048,3]{0,1:T(4,128)(2,1)S(1)}, ...), condition=%wide.region_1.2_spmd.clone, body=%wide.region_0.1_spmd.clone.sunk | while | flops 404946944 | bytes 2142293 | solution.py:19
  10.8 3.0 fusion.58
  22.0 3.0 fusion.58
  29.5 3.0 fusion.58
  36.9 3.0 fusion.58
  40.7 3.0 fusion.58
  48.2 3.0 fusion.58
  51.9 3.0 fusion.58
  55.6 3.0 fusion.58
  59.4 3.0 fusion.58
  63.1 3.0 fusion.58
  66.9 3.0 fusion.58
  69.8 9.5 %copy.52 = f32[96,16,4,256]{3,2,1,0:T(4,128)} copy(f32[96,16,4,256]{3,0,2,1:T(8,128)} %bitcast.279) | data formatting | bytes 12582912 | tf_op jit(solution)/shard_map/transpose | solution.py:20
  79.3 7.7 %reshape_reshape.9 = f32[32,3,64,256]{3,2,1,0:T(8,128)} reshape(f32[96,16,4,256]{3,2,1,0:T(4,128)} %copy.52) | data formatting | bytes 12582912 | tf_op jit(solution)/shard_map/reshape;reshape | solution.py:66
  91.2 9.2 %reduce-window.6 = s32[32,16,128]{2,1,0:T(8,128)S(1)} reduce-window(s32[32,16,128]{2,1,0:T(8,128)S(1)} %fusion.28, s32[]{:T(128)} %copy.84), window={size=1x1x128 pad=0_0x0_0x127_0}, to_apply=%region_3.4 | reduce-window | flops 8323072 | bytes 524292 | tf_op jit(solution)/shard_map/reduce-window
  101.3 4.6 %compare_select_fusion.5 = (s32[2048,1]{0,1:T(1,128)S(1)}, s32[2048,1]{0,1:T(1,128)S(1)}) fusion(s32[]{:T(128)} %bitcast.205, s32[]{:T(128)} %bitcast.206, s32[]{:T(128)} %bitcast.207, s32[]{:T(128)} %bitcast.208, s32[]{:T(128)} %bitcast.209, s32[]{:T(128)} %bitcast.211, s32[]{:T(128)} %bitcast.210, s32[2048,1]{0,1:T(1,128)S(1)} %copy-done.5), kind=kLoop, calls=%fused_computation.189 | loop fusion | flops 34816 | bytes 24604 | tf_op jit(solution)/shard_map/gather | solution.py:61
  105.9 8.8 %compare_select_fusion.29 = (s32[2048,1]{0,1:T(1,128)S(1)}, s32[2048,1]{0,1:T(1,128)S(1)}, s32[2048,1]{0,1:T(1,128)S(1)}, s32[2048,1]{0,1:T(1,128)S(1)}, s32[2048,1]{0,1:T(1,128)S(1)}, /*index=5*/s32[2048,1]{0,1:T(1,128)S(1)}) fusion(s32[]{:T(128)} %bitcast.139, s32[]{:T(128)} %bitcast.140, s32[]{:T(128)} %bitcast.141, s32[]{:T(128)} %bitcast.142, ...), kind=kLoop, calls=%fused_computation.213 | loop fusion | flops 98304 | bytes 73784 | tf_op jit(solution)/shard_map/gather | solution.py:58
  116.1 4.6 %compare_select_fusion.17 = s32[2048,1]{0,1:T(1,128)S(1)} fusion(s32[2048,1]{0,1:T(1,128)S(1)} %get-tuple-element.257, s32[]{:T(128)} %bitcast.205, s32[]{:T(128)} %bitcast.206, s32[]{:T(128)} %bitcast.207, s32[]{:T(128)} %bitcast.208, s32[]{:T(128)} %bitcast.209, s32[]{:T(128)} %bitcast.211, s32[]{:T(128)} %bitcast.210), kind=kLoop, calls=%fused_computation.201 | loop fusion | flops 24576 | bytes 16412 | tf_op jit(solution)/shard_map/gather | solution.py:62
  127.9 4.2 compare_select_fusion.28
  132.1 15.5 %select_select_fusion.5 = s32[2048]{0:T(1024)S(1)} fusion(pred[2048]{0:T(1024)(128)(4,1)S(1)} %get-tuple-element.113, pred[2048]{0:T(1024)(128)(4,1)S(1)} %get-tuple-element.112, pred[2048]{0:T(1024)(128)(4,1)S(1)} %get-tuple-element.111, pred[2048]{0:T(1024)(128)(4,1)S(1)} %get-tuple-element.110, pred[2048]{0:T(1024)(128)(4,1)S(1)} %get-tuple-element.109, ...), kind=kLoop, calls=%fused_computation.243 | loop fusion | flops 51200 | bytes 67684 | tf_op jit(solution)/shard_map/gather | solution.py:52
  147.7 35.8 %select_select_fusion.3 = s32[2048]{0:T(1024)S(1)} fusion(pred[2048]{0:T(1024)(128)(4,1)S(1)} %get-tuple-element.170, pred[2048]{0:T(1024)(128)(4,1)S(1)} %get-tuple-element.169, pred[2048]{0:T(1024)(128)(4,1)S(1)} %get-tuple-element.168, pred[2048]{0:T(1024)(128)(4,1)S(1)} %get-tuple-element.167, pred[2048]{0:T(1024)(128)(4,1)S(1)} %get-tuple-element.166, ...), kind=kLoop, calls=%fused_computation.241 | loop fusion | flops 116736 | bytes 133348 | tf_op jit(solution)/shard_map/gather | solution.py:52
  183.5 35.8 %select_select_fusion.4 = s32[2048]{0:T(1024)S(1)} fusion(pred[2048]{0:T(1024)(128)(4,1)S(1)} %get-tuple-element.227, pred[2048]{0:T(1024)(128)(4,1)S(1)} %get-tuple-element.226, pred[2048]{0:T(1024)(128)(4,1)S(1)} %get-tuple-element.225, pred[2048]{0:T(1024)(128)(4,1)S(1)} %get-tuple-element.224, pred[2048]{0:T(1024)(128)(4,1)S(1)} %get-tuple-element.223, ...), kind=kLoop, calls=%fused_computation.242 | loop fusion | flops 116736 | bytes 133348 | tf_op jit(solution)/shard_map/gather | solution.py:52
  219.6 14.4 %psum.7 = f32[3,2048]{1,0:T(4,128)S(1)} all-reduce(f32[3,2048]{1,0:T(4,128)S(1)} %convert_element_type.50), channel_id=1, replica_groups=mesh['rows'=32,'feat'=4] {'feat'}, use_global_device_ids=true, to_apply=%region_8.9 | all-reduce | flops 6144 | bytes 49152 | tf_op jit(solution)/shard_map/psum | solution.py:57
  234.0 35.7 %select_select_fusion = s32[2048]{0:T(1024)S(1)} fusion(pred[2048]{0:T(1024)(128)(4,1)S(1)} %get-tuple-element.227, pred[2048]{0:T(1024)(128)(4,1)S(1)} %get-tuple-element.226, pred[2048]{0:T(1024)(128)(4,1)S(1)} %get-tuple-element.225, pred[2048]{0:T(1024)(128)(4,1)S(1)} %get-tuple-element.224, pred[2048]{0:T(1024)(128)(4,1)S(1)} %get-tuple-element.223, ...), kind=kLoop, calls=%fused_computation.238 | loop fusion | flops 116736 | bytes 133348 | tf_op jit(solution)/shard_map/gather | solution.py:62
  269.8 35.7 %select_select_fusion.1 = s32[2048]{0:T(1024)S(1)} fusion(pred[2048]{0:T(1024)(128)(4,1)S(1)} %get-tuple-element.170, pred[2048]{0:T(1024)(128)(4,1)S(1)} %get-tuple-element.169, pred[2048]{0:T(1024)(128)(4,1)S(1)} %get-tuple-element.168, pred[2048]{0:T(1024)(128)(4,1)S(1)} %get-tuple-element.167, pred[2048]{0:T(1024)(128)(4,1)S(1)} %get-tuple-element.166, ...), kind=kLoop, calls=%fused_computation.239 | loop fusion | flops 116736 | bytes 133348 | tf_op jit(solution)/shard_map/gather | solution.py:61
  305.5 15.7 %select_select_fusion.2 = s32[2048]{0:T(1024)S(1)} fusion(pred[2048]{0:T(1024)(128)(4,1)S(1)} %get-tuple-element.113, pred[2048]{0:T(1024)(128)(4,1)S(1)} %get-tuple-element.112, pred[2048]{0:T(1024)(128)(4,1)S(1)} %get-tuple-element.111, pred[2048]{0:T(1024)(128)(4,1)S(1)} %get-tuple-element.110, pred[2048]{0:T(1024)(128)(4,1)S(1)} %get-tuple-element.109, ...), kind=kLoop, calls=%fused_computation.240 | loop fusion | flops 51200 | bytes 67684 | tf_op jit(solution)/shard_map/gather | solution.py:58
  321.6 6.1 %scatter_custom_fusion.1 = bf16[4,4096]{0,1:T(8,128)(2,1)S(1)} fusion(s32[2048]{0:T(1024)S(1)} %bitcast.303, bf16[2048,4]{1,0:T(8,128)(2,1)S(1)} %copy.58, bf16[]{:T(256)} %constant.69.clone.1), kind=kCustom, calls=%fused_computation.24 | custom fusion | bytes 32770 | tf_op jit(solution)/shard_map/scatter | solution.py:78
  328.7 12.3 %all-to-all-start.1 = ((bf16[4,32,128]{2,0,1:T(4,128)(2,1)}), bf16[4,32,128]{2,0,1:T(4,128)(2,1)S(1)}, u32[]{:S(2)}, u32[]{:S(2)}) async-start(bf16[4,32,128]{2,0,1:T(4,128)(2,1)} %copy.59), calls=%async_computation.2 | async-start | bytes 65536 | tf_op jit(solution)/shard_map/all_to_all | solution.py:84
  341.4 6.1 %scatter_custom_fusion = bf16[64,4096]{0,1:T(8,128)(2,1)S(1)} fusion(s32[2048]{0:T(1024)S(1)} %bitcast.304, bf16[2048,64]{1,0:T(8,128)(2,1)S(1)} %copy.55, bf16[]{:T(256)} %constant.69.clone.1), kind=kCustom, calls=%fused_computation.26 | custom fusion | bytes 524290 | tf_op jit(solution)/shard_map/scatter | solution.py:74
  348.6 7.4 %all-to-all-start = ((bf16[64,32,128]{2,0,1:T(8,128)(2,1)}), bf16[64,32,128]{2,0,1:T(8,128)(2,1)S(1)}, u32[]{:S(2)}, u32[]{:S(2)}) async-start(bf16[64,32,128]{2,0,1:T(8,128)(2,1)} %copy.56), calls=%async_computation.1 | async-start | bytes 1048576 | tf_op jit(solution)/shard_map/all_to_all | solution.py:83
  356.1 11.5 %all-to-all-done = bf16[64,32,128]{2,0,1:T(8,128)(2,1)S(1)} async-done(((bf16[64,32,128]{2,0,1:T(8,128)(2,1)}), bf16[64,32,128]{2,0,1:T(8,128)(2,1)S(1)}, u32[]{:S(2)}, u32[]{:S(2)}) %all-to-all-start) | async-done | bytes 524320 | tf_op jit(solution)/shard_map/all_to_all | solution.py:83
  368.1 60.7 %while.23 = (s32[]{:T(128)}, f32[16,12,4,256]{3,1,2,0:T(8,128)S(1)}, bf16[16,4,4096]{2,1,0:T(4,128)(2,1)S(1)}, bf16[4096,3]{0,1:T(4,128)(2,1)S(1)}, pred[4096,4]{0,1:T(4,128)(4,1)S(1)}, /*index=5*/s32[]{:T(128)}) while((s32[]{:T(128)}, f32[16,12,4,256]{3,1,2,0:T(8,128)S(1)}, bf16[16,4,4096]{2,1,0:T(4,128)(2,1)S(1)}, ...), condition=%wide.region_11.12_spmd.clone, body=%wide.region_10.11_spmd.clone.sunk | while | flops 104907008 | bytes 631893 | solution.py:19
  368.3 3.5 fusion.61
  372.1 3.5 fusion.61
  375.9 3.5 fusion.61
  379.7 3.5 fusion.61
  383.5 3.5 fusion.61
  387.3 3.5 fusion.61
  391.1 3.5 fusion.61
  394.9 3.5 fusion.61
  398.7 3.5 fusion.61
  402.5 3.5 fusion.61
  406.3 3.5 fusion.61
  410.1 3.5 fusion.61
  413.8 3.5 fusion.61
  417.6 3.5 fusion.61
  421.4 3.5 fusion.61
  425.2 3.5 fusion.61
  (186 shorter events, 53.4 us)
Async XLA Ops:
  7.2 424.4 %reduce-scatter.2.cloned.1.call-start = ((), (), s32[]{:S(2)}) async-start(), calls=%async_computation.3 | async-start | bytes 6488064 | tf_op jit(solution)/shard_map/reduce_scatter | solution.py:67
  87.0 0.7 copy-start.2
  87.0 2.1 copy-start.1
  87.0 3.5 copy-start.4
  87.0 4.2 copy-start.5
  87.0 38.1 %copy-start.3 = (s32[32]{0:T(128)S(1)}, s32[32]{0:T(128)}, u32[]{:S(2)}) copy-start(s32[32]{0:T(128)} %param.18) | copy-start | bytes 388
  87.0 132.4 %copy-start = (s32[2048,64]{0,1:T(8,128)S(1)}, s32[2048,64]{0,1:T(8,128)}, u32[]{:S(2)}) copy-start(s32[2048,64]{0,1:T(8,128)} %param.13) | copy-start | bytes 1572868
  328.7 19.9 %all-to-all-start.1 = ((bf16[4,32,128]{2,0,1:T(4,128)(2,1)}), bf16[4,32,128]{2,0,1:T(4,128)(2,1)S(1)}, u32[]{:S(2)}, u32[]{:S(2)}) async-start(bf16[4,32,128]{2,0,1:T(4,128)(2,1)} %copy.59), calls=%async_computation.2 | async-start | bytes 65536 | tf_op jit(solution)/shard_map/all_to_all | solution.py:84
  348.6 19.0 %all-to-all-start = ((bf16[64,32,128]{2,0,1:T(8,128)(2,1)}), bf16[64,32,128]{2,0,1:T(8,128)(2,1)S(1)}, u32[]{:S(2)}, u32[]{:S(2)}) async-start(bf16[64,32,128]{2,0,1:T(8,128)(2,1)} %copy.56), calls=%async_computation.1 | async-start | bytes 1048576 | tf_op jit(solution)/shard_map/all_to_all | solution.py:83
Sparse Core Ops, SparseCore 0:
  87.2 88.0 reduce-scatter.1
where the time goes:
time: 442 us; the launch traced here: 438 us
  other arithmetic  221 us (50%)
  matrix products  104 us (24%)
  local copies, waits for them, and re-layouts  52.5 us (12%)
  starting transfers between devices  19.8 us (4%)
  blocking collectives  14.4 us (3%)
  between operations  14.4 us (3%)
  waiting for transfers between devices  11.5 us (3%)
    dot_general x32, matrix products, one_block(): jnp.einsum('sc,fsb->cfb', weighted, table, preferred_element_type=jnp.flo...  104 us
    gather x2, other arithmetic, on_device(): child_cutoff[first_child + 1]  40.3 us
    gather x2, other arithmetic, on_device(): child_cutoff[first_child]  40.3 us
    gather x2, other arithmetic, on_device(): child_feature[first_child]  37.3 us
    gather x2, other arithmetic, on_device(): child_feature[first_child + 1]  37.3 us
    gather x2, other arithmetic, on_device(): right_root = (split_values[0] > root_cutoff[tree_node]).astype(jnp.int32)  24.5 us
    gather x3, other arithmetic, on_device(): root_feature[tree_node]  20.4 us
    psum x1, blocking collectives, on_device(): lax.psum(picked.astype(jnp.float32), 'feat').astype(jnp.int32)  14.4 us
  transfers between devices with their start and end apart: 3, of which 1 were waited for; matrix products, arithmetic and copies ran while one was open for 68% of the time, Pallas kernels for 0%

commit v1 on v0

--- a/solution.py
+++ b/solution.py
@@ -81,7 +81,12 @@
     moment_buffer = moment_buffer.reshape(4, owners, per_owner * capacity)
     got_feat, got_moment = (
         lax.all_to_all(feat_buffer, "rows", split_axis=1, concat_axis=1, tiled=True),
-        lax.all_to_all(moment_buffer, "rows", split_axis=1, concat_axis=1, tiled=True),
+        jnp.concatenate(
+            lax.all_to_all(
+                jnp.stack(jnp.split(moment_buffer, lax.axis_size("rows"), axis=1)), "rows", 0, 0
+            ),
+            axis=1,
+        ),
     )
     slots = owners * per_owner * capacity
     got_feat = got_feat.reshape(feat_here, slots)

time: 442 us -> 462 us (1.045)
  local copies, waits for them, and re-layouts: 52.5 us -> 72.6 us
    unnamed x12 -> x75, local copies, waits for them, and re-layouts: 0.62 us -> 21.1 us
  transfers between devices with their start and end apart: 3 -> 3, of which waited for: 1 -> 1; matrix products, arithmetic and copies ran while one was open for 68% -> 69% of each run, Pallas kernels for 0% -> 0%
where the time goes in v1:
time: 462 us; the launch traced here: 459 us
  other arithmetic  221 us (48%)
  matrix products  104 us (23%)
  local copies, waits for them, and re-layouts  72.6 us (16%)
  starting transfers between devices  19.8 us (4%)
  between operations  14.5 us (3%)
  blocking collectives  14.4 us (3%)
  waiting for transfers between devices  11.5 us (2%)
    dot_general x32, matrix products, one_block(): jnp.einsum('sc,fsb->cfb', weighted, table, preferred_element_type=jnp.flo...  104 us
    gather x2, other arithmetic, on_device(): child_cutoff[first_child + 1]  40.3 us
    gather x2, other arithmetic, on_device(): child_cutoff[first_child]  40.3 us
    gather x2, other arithmetic, on_device(): child_feature[first_child]  37.3 us
    gather x2, other arithmetic, on_device(): child_feature[first_child + 1]  37.3 us
    gather x2, other arithmetic, on_device(): right_root = (split_values[0] > root_cutoff[tree_node]).astype(jnp.int32)  24.5 us
    unnamed x75, local copies, waits for them, and re-layouts  21.1 us
    gather x3, other arithmetic, on_device(): root_feature[tree_node]  20.4 us
  transfers between devices with their start and end apart: 3, of which 1 were waited for; matrix products, arithmetic and copies ran while one was open for 69% of the time, Pallas kernels for 0%

profile of v1, /device:TPU:1, one launch (start us, length us, event | category | flops | bytes accessed | tf_op | source)
XLA Modules:
  0.0 458.5 jit_solution(17321333931103441368)
XLA Ops:
  10.0 59.8 %while.22 = (s32[]{:T(128)}, f32[16,96,4,256]{3,1,2,0:T(8,128)}, s32[16,4,2048]{2,1,0:T(4,128)S(1)}, bf16[2048,3]{0,1:T(4,128)(2,1)S(1)}, pred[2048,32]{0,1:T(8,128)(4,1)S(1)}, /*index=5*/s32[]{:T(128)}) while((s32[]{:T(128)}, f32[16,96,4,256]{3,1,2,0:T(8,128)}, s32[16,4,2048]{2,1,0:T(4,128)S(1)}, bf16[2048,3]{0,1:T(4,128)(2,1)S(1)}, ...), condition=%wide.region_1.2_spmd.clone, body=%wide.region_0.1_spmd.clone.sunk | while | flops 404946944 | bytes 2142293 | solution.py:19
  10.8 3.0 fusion.60
  22.0 3.0 fusion.60
  29.5 3.0 fusion.60
  36.9 3.0 fusion.60
  40.7 3.0 fusion.60
  48.2 3.0 fusion.60
  51.9 3.0 fusion.60
  55.6 3.0 fusion.60
  59.4 3.0 fusion.60
  63.1 3.0 fusion.60
  66.9 3.0 fusion.60
  69.8 9.5 %copy.184 = f32[96,16,4,256]{3,2,1,0:T(4,128)} copy(f32[96,16,4,256]{3,0,2,1:T(8,128)} %bitcast.340) | data formatting | bytes 12582912 | tf_op jit(solution)/shard_map/transpose | solution.py:20
  79.3 7.7 %reshape_reshape.10 = f32[32,3,64,256]{3,2,1,0:T(8,128)} reshape(f32[96,16,4,256]{3,2,1,0:T(4,128)} %copy.184) | data formatting | bytes 12582912 | tf_op jit(solution)/shard_map/reshape;reshape | solution.py:66
  91.2 9.2 %reduce-window.6 = s32[32,16,128]{2,1,0:T(8,128)S(1)} reduce-window(s32[32,16,128]{2,1,0:T(8,128)S(1)} %fusion.28, s32[]{:T(128)} %copy.305), window={size=1x1x128 pad=0_0x0_0x127_0}, to_apply=%region_3.4 | reduce-window | flops 8323072 | bytes 524292 | tf_op jit(solution)/shard_map/reduce-window
  101.3 4.6 compare_select_fusion.5
  105.9 8.8 %compare_select_fusion.29 = (s32[2048,1]{0,1:T(1,128)S(1)}, s32[2048,1]{0,1:T(1,128)S(1)}, s32[2048,1]{0,1:T(1,128)S(1)}, s32[2048,1]{0,1:T(1,128)S(1)}, s32[2048,1]{0,1:T(1,128)S(1)}, /*index=5*/s32[2048,1]{0,1:T(1,128)S(1)}) fusion(s32[]{:T(128)} %bitcast.139, s32[]{:T(128)} %bitcast.140, s32[]{:T(128)} %bitcast.141, s32[]{:T(128)} %bitcast.142, ...), kind=kLoop, calls=%fused_computation.245 | loop fusion | flops 98304 | bytes 73784 | tf_op jit(solution)/shard_map/gather | solution.py:58
  116.1 4.6 compare_select_fusion.17
  127.9 4.2 compare_select_fusion.28
  132.1 15.5 %select_select_fusion.5 = s32[2048]{0:T(1024)S(1)} fusion(pred[2048]{0:T(1024)(128)(4,1)S(1)} %get-tuple-element.113, pred[2048]{0:T(1024)(128)(4,1)S(1)} %get-tuple-element.112, pred[2048]{0:T(1024)(128)(4,1)S(1)} %get-tuple-element.111, pred[2048]{0:T(1024)(128)(4,1)S(1)} %get-tuple-element.110, pred[2048]{0:T(1024)(128)(4,1)S(1)} %get-tuple-element.109, ...), kind=kLoop, calls=%fused_computation.275 | loop fusion | flops 51200 | bytes 67684 | tf_op jit(solution)/shard_map/gather | solution.py:52
  147.7 35.8 %select_select_fusion.3 = s32[2048]{0:T(1024)S(1)} fusion(pred[2048]{0:T(1024)(128)(4,1)S(1)} %get-tuple-element.170, pred[2048]{0:T(1024)(128)(4,1)S(1)} %get-tuple-element.169, pred[2048]{0:T(1024)(128)(4,1)S(1)} %get-tuple-element.168, pred[2048]{0:T(1024)(128)(4,1)S(1)} %get-tuple-element.167, pred[2048]{0:T(1024)(128)(4,1)S(1)} %get-tuple-element.166, ...), kind=kLoop, calls=%fused_computation.273 | loop fusion | flops 116736 | bytes 133348 | tf_op jit(solution)/shard_map/gather | solution.py:52
  183.5 35.8 %select_select_fusion.4 = s32[2048]{0:T(1024)S(1)} fusion(pred[2048]{0:T(1024)(128)(4,1)S(1)} %get-tuple-element.227, pred[2048]{0:T(1024)(128)(4,1)S(1)} %get-tuple-element.226, pred[2048]{0:T(1024)(128)(4,1)S(1)} %get-tuple-element.225, pred[2048]{0:T(1024)(128)(4,1)S(1)} %get-tuple-element.224, pred[2048]{0:T(1024)(128)(4,1)S(1)} %get-tuple-element.223, ...), kind=kLoop, calls=%fused_computation.274 | loop fusion | flops 116736 | bytes 133348 | tf_op jit(solution)/shard_map/gather | solution.py:52
  219.6 14.4 %psum.7 = f32[3,2048]{1,0:T(4,128)S(1)} all-reduce(f32[3,2048]{1,0:T(4,128)S(1)} %convert_element_type.50), channel_id=1, replica_groups=mesh['rows'=32,'feat'=4] {'feat'}, use_global_device_ids=true, to_apply=%region_8.9 | all-reduce | flops 6144 | bytes 49152 | tf_op jit(solution)/shard_map/psum | solution.py:57
  234.0 35.7 %select_select_fusion = s32[2048]{0:T(1024)S(1)} fusion(pred[2048]{0:T(1024)(128)(4,1)S(1)} %get-tuple-element.227, pred[2048]{0:T(1024)(128)(4,1)S(1)} %get-tuple-element.226, pred[2048]{0:T(1024)(128)(4,1)S(1)} %get-tuple-element.225, pred[2048]{0:T(1024)(128)(4,1)S(1)} %get-tuple-element.224, pred[2048]{0:T(1024)(128)(4,1)S(1)} %get-tuple-element.223, ...), kind=kLoop, calls=%fused_computation.270 | loop fusion | flops 116736 | bytes 133348 | tf_op jit(solution)/shard_map/gather | solution.py:62
  269.8 35.7 %select_select_fusion.1 = s32[2048]{0:T(1024)S(1)} fusion(pred[2048]{0:T(1024)(128)(4,1)S(1)} %get-tuple-element.170, pred[2048]{0:T(1024)(128)(4,1)S(1)} %get-tuple-element.169, pred[2048]{0:T(1024)(128)(4,1)S(1)} %get-tuple-element.168, pred[2048]{0:T(1024)(128)(4,1)S(1)} %get-tuple-element.167, pred[2048]{0:T(1024)(128)(4,1)S(1)} %get-tuple-element.166, ...), kind=kLoop, calls=%fused_computation.271 | loop fusion | flops 116736 | bytes 133348 | tf_op jit(solution)/shard_map/gather | solution.py:61
  305.5 15.7 %select_select_fusion.2 = s32[2048]{0:T(1024)S(1)} fusion(pred[2048]{0:T(1024)(128)(4,1)S(1)} %get-tuple-element.113, pred[2048]{0:T(1024)(128)(4,1)S(1)} %get-tuple-element.112, pred[2048]{0:T(1024)(128)(4,1)S(1)} %get-tuple-element.111, pred[2048]{0:T(1024)(128)(4,1)S(1)} %get-tuple-element.110, pred[2048]{0:T(1024)(128)(4,1)S(1)} %get-tuple-element.109, ...), kind=kLoop, calls=%fused_computation.272 | loop fusion | flops 51200 | bytes 67684 | tf_op jit(solution)/shard_map/gather | solution.py:58
  321.6 6.1 %scatter_custom_fusion.1 = bf16[4,4096]{0,1:T(8,128)(2,1)S(1)} fusion(s32[2048]{0:T(1024)S(1)} %bitcast.368, bf16[2048,4]{1,0:T(8,128)(2,1)S(1)} %copy.190, bf16[]{:T(256)} %constant.69.clone.1), kind=kCustom, calls=%fused_computation.24 | custom fusion | bytes 32770 | tf_op jit(solution)/shard_map/scatter | solution.py:78
  348.9 12.3 %all-to-all-start.1 = ((bf16[32,4,1,128]{3,1,2,0:T(4,128)(2,1)}), bf16[32,4,1,128]{3,1,2,0:T(4,128)(2,1)S(1)}, u32[]{:S(2)}, u32[]{:S(2)}) async-start(bf16[32,4,1,128]{3,1,2,0:T(4,128)(2,1)} %constant_dynamic-update-slice_fusion), calls=%async_computation.2 | async-start | bytes 65536 | tf_op jit(solution)/shard_map/all_to_all | solution.py:85
  361.5 6.1 %scatter_custom_fusion = bf16[64,4096]{0,1:T(8,128)(2,1)S(1)} fusion(s32[2048]{0:T(1024)S(1)} %bitcast.369, bf16[2048,64]{1,0:T(8,128)(2,1)S(1)} %copy.187, bf16[]{:T(256)} %constant.69.clone.1), kind=kCustom, calls=%fused_computation.26 | custom fusion | bytes 524290 | tf_op jit(solution)/shard_map/scatter | solution.py:74
  368.7 7.4 %all-to-all-start = ((bf16[64,32,128]{2,0,1:T(8,128)(2,1)}), bf16[64,32,128]{2,0,1:T(8,128)(2,1)S(1)}, u32[]{:S(2)}, u32[]{:S(2)}) async-start(bf16[64,32,128]{2,0,1:T(8,128)(2,1)} %copy.188), calls=%async_computation.1 | async-start | bytes 1048576 | tf_op jit(solution)/shard_map/all_to_all | solution.py:83
  376.2 11.5 %all-to-all-done = bf16[64,32,128]{2,0,1:T(8,128)(2,1)S(1)} async-done(((bf16[64,32,128]{2,0,1:T(8,128)(2,1)}), bf16[64,32,128]{2,0,1:T(8,128)(2,1)S(1)}, u32[]{:S(2)}, u32[]{:S(2)}) %all-to-all-start) | async-done | bytes 524320 | tf_op jit(solution)/shard_map/all_to_all | solution.py:83
  388.2 60.7 %while.23 = (s32[]{:T(128)}, f32[16,12,4,256]{3,1,2,0:T(8,128)S(1)}, bf16[16,4,4096]{2,1,0:T(4,128)(2,1)S(1)}, bf16[4096,3]{0,1:T(4,128)(2,1)S(1)}, pred[4096,4]{0,1:T(4,128)(4,1)S(1)}, /*index=5*/s32[]{:T(128)}) while((s32[]{:T(128)}, f32[16,12,4,256]{3,1,2,0:T(8,128)S(1)}, bf16[16,4,4096]{2,1,0:T(4,128)(2,1)S(1)}, ...), condition=%wide.region_11.12_spmd.clone, body=%wide.region_10.11_spmd.clone.sunk | while | flops 104907008 | bytes 631893 | solution.py:19
  388.5 3.5 fusion.63
  392.3 3.5 fusion.63
  396.1 3.5 fusion.63
  399.9 3.5 fusion.63
  403.7 3.5 fusion.63
  407.5 3.5 fusion.63
  411.2 3.5 fusion.63
  415.0 3.5 fusion.63
  418.8 3.5 fusion.63
  422.6 3.5 fusion.63
  426.4 3.5 fusion.63
  430.2 3.5 fusion.63
  434.0 3.5 fusion.63
  437.8 3.5 fusion.63
  441.6 3.5 fusion.63
  445.4 3.5 fusion.63
  (251 shorter events, 73.6 us)
Async XLA Ops:
  7.2 444.5 %reduce-scatter.2.cloned.1.call-start = ((), (), s32[]{:S(2)}) async-start(), calls=%async_computation.3 | async-start | bytes 6488064 | tf_op jit(solution)/shard_map/reduce_scatter | solution.py:67
  87.0 0.7 copy-start.2
  87.0 2.1 copy-start.1
  87.0 3.5 copy-start.4
  87.0 4.2 copy-start.5
  87.0 38.1 %copy-start.3 = (s32[32]{0:T(128)S(1)}, s32[32]{0:T(128)}, u32[]{:S(2)}) copy-start(s32[32]{0:T(128)} %param.18) | copy-start | bytes 388
  87.0 132.4 %copy-start = (s32[2048,64]{0,1:T(8,128)S(1)}, s32[2048,64]{0,1:T(8,128)}, u32[]{:S(2)}) copy-start(s32[2048,64]{0,1:T(8,128)} %param.13) | copy-start | bytes 1572868
  348.9 19.9 %all-to-all-start.1 = ((bf16[32,4,1,128]{3,1,2,0:T(4,128)(2,1)}), bf16[32,4,1,128]{3,1,2,0:T(4,128)(2,1)S(1)}, u32[]{:S(2)}, u32[]{:S(2)}) async-start(bf16[32,4,1,128]{3,1,2,0:T(4,128)(2,1)} %constant_dynamic-update-slice_fusion), calls=%async_computation.2 | async-start | bytes 65536 | tf_op jit(solution)/shard_map/all_to_all | solution.py:85
  368.7 19.0 %all-to-all-start = ((bf16[64,32,128]{2,0,1:T(8,128)(2,1)}), bf16[64,32,128]{2,0,1:T(8,128)(2,1)S(1)}, u32[]{:S(2)}, u32[]{:S(2)}) async-start(bf16[64,32,128]{2,0,1:T(8,128)(2,1)} %copy.188), calls=%async_computation.1 | async-start | bytes 1048576 | tf_op jit(solution)/shard_map/all_to_all | solution.py:83
Sparse Core Ops, SparseCore 0:
  87.2 88.0 reduce-scatter.1
